TPU v7x, 32 devices: a whole 2x2x4 slice. The times are simulated.
32 devices in a mesh: dp: 8 (over y, x, core), mp: 4 (over z).
Axes of the slice: x: 2, y: 2, z: 4, core: 2. Of those that a mesh axis runs over, the one named last changes fastest.
Arguments:
- embeddings: bfloat16 [65536, 2560], P('dp', 'mp')
- centroids: bfloat16 [16384, 2560], P(('dp', 'mp'))
- labels: bfloat16 [16384, 1024], P(('dp', 'mp')), may hold values from -12 to 12
- candidates: int32 [256, 8], P(('dp', 'mp')), may hold values from 0 to 127, as said below
- counts: int32 [256], P(('dp', 'mp')), may hold values from 4 to 8, as said below
- home: int32 [128], replicated, may hold values from 0 to 127, as said below
Outputs:
- profiles: bfloat16 [65536, 1024], P(('dp', 'mp'))
Inputs may be any that keep to these rules, and one draw needn't show every extreme that they name: `home`: a permutation of the tiles. `candidates`: candidate tile ids are distinct within a block; entries from position counts[b] on are padding; the candidate tiles of the 8 blocks of one device, padding included, are exactly one tile stored on each device with the same mp index. `counts`: some block of every device has 8.
All inputs are finite; a program needn't handle non-finite values.
Results may differ from a plain program's by a relative error of at most 0.0048.
Values may be sent and summed in bfloat16 or wider, within the bound.
A program may use at most 192 MiB of HBM per device.

v0:
```python
import functools
import math

import jax
import jax.numpy as jnp
from jax import lax
from jax.experimental import pallas as pl
from jax.experimental.pallas import tpu as pltpu
from jax.sharding import PartitionSpec as P

TR = 128
BR = 256
UNIT = 256
MESH = pl.DeviceIdType.MESH
VMEM_BYTES = 62 * 1024 * 1024
CLOSE_BYTES = 14 * 1024 * 1024


def products(members, features):
    return lax.dot_general(
        members, features, (((1,), (1,)), ((), ())), preferred_element_type=jnp.float32
    )


def profile_of(raw, pool_ref, width, live, scale, logits):
    logits[...] = jnp.where(live > 0, raw * scale, -jnp.inf)
    values = logits[...]
    peak = jnp.max(values, axis=1, keepdims=True)
    weights = jnp.exp(values - peak)
    total = jnp.sum(weights, axis=1, keepdims=True)
    probs = (weights / total).astype(jnp.bfloat16)
    label_columns = pl.ds(width, pool_ref.shape[1] - width)
    profile = jnp.dot(probs, pool_ref[:, label_columns], preferred_element_type=jnp.float32)
    return profile.astype(jnp.bfloat16)


def close_kernel(count_mp, scale, held_ref, rows_ref, pool_ref, live_ref, near_ref, out_ref, logits, result, sem):
    done = held_ref.shape[0] // UNIT
    copies = [
        pltpu.make_async_copy(
            held_ref.at[pl.ds(i * UNIT, UNIT), :], out_ref.at[pl.ds(i * UNIT, UNIT), :], sem.at[i]
        )
        for i in range(done)
    ]
    for copy in copies:
        copy.start()
    last = pl.ds(done * UNIT, UNIT)
    width = rows_ref.shape[1]
    span = width // 2
    side = lax.axis_index("mp") // (count_mp // 2)
    far = pl.ds(pl.multiple_of((1 - side) * span, span), span)
    raw = near_ref[...] + products(rows_ref[last, far], pool_ref[:, far])
    result[...] = profile_of(raw, pool_ref, width, live_ref[pl.ds(0, 1), :], scale, logits)
    final = pltpu.make_async_copy(result, out_ref.at[last, :], sem.at[done])
    final.start()
    for copy in copies + [final]:
        copy.wait()


def kernel(
    count_dp,
    count_mp,
    scale,
    cand_hbm,
    count_hbm,
    home_hbm,
    emb_ref,
    cent_ref,
    label_ref,
    out_ref,
    rows,
    pool,
    last_live,
    last_near,
    cand_ref,
    count_ref,
    home_ref,
    stored,
    staging,
    ids_out,
    ids_in,
    logits,
    row_send,
    row_recv,
    id_send,
    id_recv,
    tile_send,
    tile_recv,
    local_sem,
):
    my_dp = lax.axis_index("dp")
    my_mp = lax.axis_index("mp")
    blocks, cands = cand_ref.shape
    units = blocks * BR // UNIT
    part = emb_ref.shape[1]
    tile_count = stored.shape[0]
    width = cent_ref.shape[2]
    label_width = label_ref.shape[2]
    slots = staging.shape[0]
    half = count_mp // 2
    side = my_mp // half
    place = my_mp % half

    barrier = pltpu.get_barrier_semaphore()
    for i in range(1, count_mp):
        pl.semaphore_signal(
            barrier, inc=1, device_id=(my_dp, (my_mp + i) % count_mp), device_id_type=MESH
        )

    def greet(i, carry):
        pl.semaphore_signal(
            barrier, inc=1, device_id=((my_dp + i) % count_dp, my_mp), device_id_type=MESH
        )
        return carry

    lax.fori_loop(1, count_dp, greet, 0)

    own_columns = pl.ds(pl.multiple_of(my_mp * part, part), part)
    here = [
        pltpu.make_async_copy(cent_ref, stored.at[:, :, pl.ds(0, width)], local_sem.at[0]),
        pltpu.make_async_copy(label_ref, stored.at[:, :, pl.ds(width, label_width)], local_sem.at[1]),
        pltpu.make_async_copy(
            emb_ref.at[pl.ds(pl.multiple_of(my_mp * blocks * BR, BR), blocks * BR), :],
            rows.at[:, own_columns],
            local_sem.at[2],
        ),
        pltpu.make_async_copy(cand_hbm, cand_ref, local_sem.at[3]),
        pltpu.make_async_copy(count_hbm, count_ref, local_sem.at[4]),
        pltpu.make_async_copy(home_hbm, home_ref, local_sem.at[5]),
    ]
    for copy in here:
        copy.start()

    pl.semaphore_wait(barrier, count_mp - 1 + count_dp - 1)

    def send_rows(b, target):
        return pltpu.make_async_remote_copy(
            src_ref=emb_ref.at[pl.ds(pl.multiple_of((target * units + b) * UNIT, UNIT), UNIT), :],
            dst_ref=rows.at[pl.ds(pl.multiple_of(b * UNIT, UNIT), UNIT), own_columns],
            send_sem=row_send.at[target, b],
            recv_sem=row_recv.at[my_mp, b],
            device_id=(my_dp, target),
            device_id_type=MESH,
        )

    near = [side * half + (place + i) % half for i in range(1, half)]
    far = [(1 - side) * half + (place + i) % half for i in range(half)]

    def send_near(b, carry):
        for target in near:
            send_rows(b, target).start()
        return carry

    def send_far(b, carry):
        for target in far:
            send_rows(b, target).start()
        return carry

    def send_id(i):
        peer = (my_dp + i) % count_dp
        return pltpu.make_async_remote_copy(
            src_ref=ids_out.at[peer],
            dst_ref=ids_in.at[my_dp],
            send_sem=id_send.at[i],
            recv_sem=id_recv.at[i],
            device_id=(peer, my_mp),
            device_id_type=MESH,
        )

    def start_id(i, carry):
        send_id(i).start()
        return carry

    lax.fori_loop(0, units, send_near, 0)
    lax.fori_loop(0, units, send_far, 0)
    for copy in here[3:]:
        copy.wait()
    peer_ids = lax.broadcasted_iota(jnp.int32, ids_out.shape, 0)

    def want(b, carry):
        for j in range(cands):
            cell = home_ref[cand_ref[b, j]]
            carry = jnp.where(peer_ids == cell // (tile_count * count_mp), cell % tile_count, carry)
        return carry

    ids_out[...] = lax.fori_loop(0, blocks, want, jnp.zeros(ids_out.shape, jnp.int32))

    for copy in here[:2]:
        copy.wait()
    lax.fori_loop(1, count_dp, start_id, 0)

    my_tile = pl.ds(pl.multiple_of(my_dp * TR, TR), TR)

    def send_tile(i):
        return pltpu.make_async_remote_copy(
            src_ref=staging.at[(i - 1) % slots],
            dst_ref=pool.at[my_tile, :],
            send_sem=tile_send.at[i],
            recv_sem=tile_recv.at[i],
            device_id=((my_dp + count_dp - i) % count_dp, my_mp),
            device_id_type=MESH,
        )

    def stage(i, carry):
        send_id(i).wait_recv()
        index = jnp.max(ids_in[(my_dp + count_dp - i) % count_dp])

        @pl.when(i > slots)
        def _():
            send_tile(i - slots).wait_send()

        staging[(i - 1) % slots] = stored[index]

        @pl.when(i > 1)
        def _():
            send_tile(i - 1).start()

        return carry

    lax.fori_loop(1, count_dp, stage, 0)
    pool[my_tile, :] = stored[jnp.max(ids_out[my_dp])]
    send_tile(count_dp - 1).start()

    def tile_arrives(i, carry):
        send_tile(i).wait_recv()
        return carry

    lax.fori_loop(1, count_dp, tile_arrives, 0)
    here[2].wait()

    def rows_arrive(b, sources):
        for source in sources:
            pltpu.make_async_remote_copy(
                src_ref=emb_ref.at[pl.ds(0, UNIT), :],
                dst_ref=rows.at[
                    pl.ds(pl.multiple_of(b * UNIT, UNIT), UNIT),
                    pl.ds(pl.multiple_of(source * part, part), part),
                ],
                send_sem=row_send.at[source, b],
                recv_sem=row_recv.at[source, b],
                device_id=(my_dp, source),
                device_id_type=MESH,
            ).wait_recv()

    def live_of(b, shape):
        block = b // (BR // UNIT)
        count = count_ref[block]
        column_peer = lax.broadcasted_iota(jnp.int32, shape, 1) // TR
        live = jnp.zeros(shape, jnp.int32)
        for j in range(cands):
            slot = home_ref[cand_ref[block, j]] // (tile_count * count_mp)
            slot = jnp.where(j < count, slot, -1)
            live = jnp.where(column_peer == slot, 1, live)
        return live

    last_live[...] = live_of(units - 1, last_live.shape)

    def score(b, carry):
        rows_arrive(b, near + far)
        mine = pl.ds(pl.multiple_of(b * UNIT, UNIT), UNIT)
        live = live_of(b, (1, count_dp * TR))
        raw = products(rows[mine, :], pool[:, pl.ds(0, width)])
        out_ref[mine, :] = profile_of(raw, pool, width, live, scale, logits)
        return carry

    lax.fori_loop(0, units - 1, score, 0)
    rows_arrive(units - 1, near)
    span = width // 2
    near_columns = pl.ds(pl.multiple_of(side * span, span), span)
    last_near[...] = products(rows[pl.ds((units - 1) * UNIT, UNIT), near_columns], pool[:, near_columns])
    rows_arrive(units - 1, far)

    def finish_rows(b, carry):
        for target in near + far:
            send_rows(b, target).wait_send()
        return carry

    lax.fori_loop(0, units, finish_rows, 0)

    def finish_ids(i, carry):
        send_id(i).wait_send()
        return carry

    lax.fori_loop(1, count_dp, finish_ids, 0)

    def finish_tiles(i, carry):
        send_tile(i).wait_send()
        return carry

    lax.fori_loop(max(count_dp - slots, 1), count_dp, finish_tiles, 0)


def body(embeddings, centroids, labels, candidates, counts, home):
    count_dp = lax.axis_size("dp")
    count_mp = lax.axis_size("mp")
    part = embeddings.shape[1]
    width = centroids.shape[1]
    label_width = labels.shape[1]
    tile_count = centroids.shape[0] // TR
    blocks, cands = candidates.shape
    row_count = blocks * BR
    units = row_count // UNIT
    both = width + label_width
    slots = count_dp - 1 if count_dp <= 8 else 3
    anywhere = pl.BlockSpec(memory_space=pl.ANY)
    local = pl.BlockSpec(memory_space=pltpu.VMEM)
    scale = 2.0 / math.sqrt(width)
    handed = [
        pltpu.VMEM((row_count - UNIT, label_width), jnp.bfloat16),
        pltpu.VMEM((row_count, width), jnp.bfloat16),
        pltpu.VMEM((count_dp * TR, both), jnp.bfloat16),
        pltpu.VMEM((8, count_dp * TR), jnp.int32),
        pltpu.VMEM((UNIT, count_dp * TR), jnp.float32),
    ]
    handed_bytes = 2 * ((row_count - UNIT) * label_width + row_count * width) + count_dp * TR * (2 * both + 32 + 4 * UNIT)
    held = pl.pallas_call(
        functools.partial(kernel, count_dp, count_mp, scale),
        in_specs=[anywhere] * 6,
        out_specs=[local] * len(handed),
        out_shape=handed,
        scratch_shapes=[
            pltpu.SMEM(candidates.shape, jnp.int32),
            pltpu.SMEM(counts.shape, jnp.int32),
            pltpu.SMEM(home.shape, jnp.int32),
            pltpu.VMEM((tile_count, TR, both), jnp.bfloat16),
            pltpu.VMEM((slots, TR, both), jnp.bfloat16),
            pltpu.VMEM((count_dp, 8, 128), jnp.int32),
            pltpu.VMEM((count_dp, 8, 128), jnp.int32),
            pltpu.VMEM((UNIT, count_dp * TR), jnp.float32),
            pltpu.SemaphoreType.DMA((count_mp, units)),
            pltpu.SemaphoreType.DMA((count_mp, units)),
            pltpu.SemaphoreType.DMA((count_dp,)),
            pltpu.SemaphoreType.DMA((count_dp,)),
            pltpu.SemaphoreType.DMA((count_dp,)),
            pltpu.SemaphoreType.DMA((count_dp,)),
            pltpu.SemaphoreType.DMA((6,)),
        ],
        compiler_params=pltpu.CompilerParams(
            collective_id=0, has_side_effects=True, vmem_limit_bytes=VMEM_BYTES - handed_bytes
        ),
        name="annotate",
    )(
        candidates,
        counts,
        home,
        embeddings,
        centroids.reshape(tile_count, TR, width),
        labels.reshape(tile_count, TR, label_width),
    )
    return pl.pallas_call(
        functools.partial(close_kernel, count_mp, scale),
        in_specs=[local] * len(handed),
        out_specs=anywhere,
        out_shape=jax.ShapeDtypeStruct((row_count, label_width), jnp.bfloat16),
        scratch_shapes=[
            pltpu.VMEM((UNIT, count_dp * TR), jnp.float32),
            pltpu.VMEM((UNIT, label_width), jnp.bfloat16),
            pltpu.SemaphoreType.DMA((units,)),
        ],
        compiler_params=pltpu.CompilerParams(vmem_limit_bytes=CLOSE_BYTES),
        name="close",
    )(*[pltpu.with_memory_space_constraint(value, pltpu.VMEM) for value in held])


def solution(mesh):
    placed = (
        P("dp", "mp"),
        P(("dp", "mp"), None),
        P(("dp", "mp"), None),
        P(("dp", "mp"), None),
        P(("dp", "mp")),
        P(),
    )
    return jax.shard_map(
        body, mesh=mesh, in_specs=placed, out_specs=P(("dp", "mp"), None), check_vma=False
    )
```

profile of v0, /device:TPU:8, one launch (start us, length us, event | category | flops | bytes accessed | tf_op | source)
XLA Modules:
  0.0 233.9 jit_solution(12697996486708293837)
XLA Ops:
  0.0 231.3 %annotate.1 = (bf16[1792,1024]{1,0:T(8,128)(2,1)S(1)}, bf16[2048,2560]{1,0:T(8,128)(2,1)S(1)}, bf16[1024,3584]{1,0:T(8,128)(2,1)S(1)}, s32[8,1024]{1,0:T(8,128)S(1)}, f32[256,1024]{1,0:T(8,128)S(1)}) custom-call(s32[8,8]{1,0:T(8,128)} %cand_hbm.1, s32[8]{0:T(128)} %count_hbm.1, s32[128]{0:T(128)} %home_hbm.1, bf16[8192,640]{1,0:T(8,128)(2,1)} %emb_ref.1, ...), custom_call_target="tpu_custom_call" | custom-call | tf_op jit(solution)/shard_map/annotate/pallas_call | solution.py:316
  231.3 2.6 %close.1 = bf16[2048,1024]{1,0:T(8,128)(2,1)} custom-call(bf16[1792,1024]{1,0:T(8,128)(2,1)S(1)} %get-tuple-element.10.held_ref, bf16[2048,2560]{1,0:T(8,128)(2,1)S(1)} %get-tuple-element.11.rows_ref, bf16[1024,3584]{1,0:T(8,128)(2,1)S(1)} %get-tuple-element.12.pool_ref, s32[8,1024]{1,0:T(8,128)S(1)} %get-tuple-element.13.live_ref, ...), custom_call_target="tpu_custom_call" | custom-call | tf_op jit(solution)/shard_map/close/pallas_call | solution.py:350
where the time goes:
time: 234 us
  Pallas kernels  234 us (100%)
    pallas_call x1, Pallas kernels, body(): pl.pallas_call(functools.partial(kernel, count_dp, count_mp, scale), in_s...  231 us

commit v1 on v0

--- a/solution.py
+++ b/solution.py
@@ -11,6 +11,8 @@
 TR = 128
 BR = 256
 UNIT = 256
+TAIL = (128, 64, 64)
+EARLY = 2
 MESH = pl.DeviceIdType.MESH
 VMEM_BYTES = 62 * 1024 * 1024
 CLOSE_BYTES = 14 * 1024 * 1024
@@ -23,8 +25,9 @@
 
 
 def profile_of(raw, pool_ref, width, live, scale, logits):
-    logits[...] = jnp.where(live > 0, raw * scale, -jnp.inf)
-    values = logits[...]
+    here = pl.ds(0, raw.shape[0])
+    logits[here, :] = jnp.where(live > 0, raw * scale, -jnp.inf)
+    values = logits[here, :]
     peak = jnp.max(values, axis=1, keepdims=True)
     weights = jnp.exp(values - peak)
     total = jnp.sum(weights, axis=1, keepdims=True)
@@ -34,24 +37,30 @@
     return profile.astype(jnp.bfloat16)
 
 
-def close_kernel(count_mp, scale, held_ref, rows_ref, pool_ref, live_ref, near_ref, out_ref, logits, result, sem):
-    done = held_ref.shape[0] // UNIT
+def pieces_of(row_count):
+    whole = row_count - sum(TAIL)
+    sizes = [UNIT] * (whole // UNIT) + list(TAIL)
+    starts = [sum(sizes[:i]) for i in range(len(sizes))]
+    return list(zip(starts, sizes))
+
+
+def close_kernel(count_mp, scale, held_ref, rows_ref, pool_ref, live_ref, rest_ref, out_ref, logits, result, sem):
+    pieces = pieces_of(out_ref.shape[0])
     copies = [
-        pltpu.make_async_copy(
-            held_ref.at[pl.ds(i * UNIT, UNIT), :], out_ref.at[pl.ds(i * UNIT, UNIT), :], sem.at[i]
-        )
-        for i in range(done)
+        pltpu.make_async_copy(held_ref.at[pl.ds(*piece), :], out_ref.at[pl.ds(*piece), :], sem.at[i])
+        for i, piece in enumerate(pieces[:-1])
     ]
     for copy in copies:
         copy.start()
-    last = pl.ds(done * UNIT, UNIT)
+    last = pl.ds(*pieces[-1])
     width = rows_ref.shape[1]
-    span = width // 2
-    side = lax.axis_index("mp") // (count_mp // 2)
-    far = pl.ds(pl.multiple_of((1 - side) * span, span), span)
-    raw = near_ref[...] + products(rows_ref[last, far], pool_ref[:, far])
+    part = width // count_mp
+    half = count_mp // 2
+    side = lax.axis_index("mp") // half
+    late = pl.ds(pl.multiple_of((half - side) * part, part), part)
+    raw = rest_ref[...] + products(rows_ref[last, late], pool_ref[:, late])
     result[...] = profile_of(raw, pool_ref, width, live_ref[pl.ds(0, 1), :], scale, logits)
-    final = pltpu.make_async_copy(result, out_ref.at[last, :], sem.at[done])
+    final = pltpu.make_async_copy(result, out_ref.at[last, :], sem.at[len(copies)])
     final.start()
     for copy in copies + [final]:
         copy.wait()
@@ -71,7 +80,7 @@
     rows,
     pool,
     last_live,
-    last_near,
+    last_rest,
     cand_ref,
     count_ref,
     home_ref,
@@ -84,6 +93,7 @@
     row_recv,
     id_send,
     id_recv,
+    ready,
     tile_send,
     tile_recv,
     local_sem,
@@ -91,7 +101,8 @@
     my_dp = lax.axis_index("dp")
     my_mp = lax.axis_index("mp")
     blocks, cands = cand_ref.shape
-    units = blocks * BR // UNIT
+    pieces = pieces_of(blocks * BR)
+    units = len(pieces) - len(TAIL)
     part = emb_ref.shape[1]
     tile_count = stored.shape[0]
     width = cent_ref.shape[2]
@@ -101,19 +112,41 @@
     side = my_mp // half
     place = my_mp % half
 
+    edge = half - 1 + side
+    opposite = half - side
+    at_edge = my_mp == edge
+    outers = [side * (half + 1) + i for i in range(half - 1)]
+    others = [(1 - side) * (half + 1) + i for i in range(half - 1)]
     barrier = pltpu.get_barrier_semaphore()
-    for i in range(1, count_mp):
-        pl.semaphore_signal(
-            barrier, inc=1, device_id=(my_dp, (my_mp + i) % count_mp), device_id_type=MESH
-        )
-
-    def greet(i, carry):
-        pl.semaphore_signal(
-            barrier, inc=1, device_id=((my_dp + i) % count_dp, my_mp), device_id_type=MESH
-        )
-        return carry
-
-    lax.fori_loop(1, count_dp, greet, 0)
+
+    def tell(dp, mp):
+        pl.semaphore_signal(barrier, inc=1, device_id=(dp, mp), device_id_type=MESH)
+
+    @pl.when(at_edge)
+    def _():
+        tell(my_dp, opposite)
+        for mp in outers + others:
+            tell(my_dp, mp)
+
+        def greet(i, carry):
+            for mp in outers:
+                tell((my_dp + i) % count_dp, mp)
+            return carry
+
+        lax.fori_loop(1, count_dp, greet, 0)
+
+    @pl.when(jnp.logical_not(at_edge))
+    def _():
+        for mp in others:
+            tell(my_dp, mp)
+        for i in range(1, half - 1):
+            tell(my_dp, side * (half + 1) + (my_mp - side * (half + 1) + i) % (half - 1))
+
+        def greet(i, carry):
+            tell((my_dp + i) % count_dp, my_mp)
+            return carry
+
+        lax.fori_loop(1, count_dp, greet, 0)
 
     own_columns = pl.ds(pl.multiple_of(my_mp * part, part), part)
     here = [
@@ -131,12 +164,13 @@
     for copy in here:
         copy.start()
 
-    pl.semaphore_wait(barrier, count_mp - 1 + count_dp - 1)
-
-    def send_rows(b, target):
+    pl.semaphore_wait(barrier, jnp.where(at_edge, 1, count_mp - 1 + 2 * (count_dp - 1)))
+
+    def send_rows(piece, b, target):
+        start, size = piece
         return pltpu.make_async_remote_copy(
-            src_ref=emb_ref.at[pl.ds(pl.multiple_of((target * units + b) * UNIT, UNIT), UNIT), :],
-            dst_ref=rows.at[pl.ds(pl.multiple_of(b * UNIT, UNIT), UNIT), own_columns],
+            src_ref=emb_ref.at[pl.ds(pl.multiple_of(target * blocks * BR + start, size), size), :],
+            dst_ref=rows.at[pl.ds(pl.multiple_of(start, size), size), own_columns],
             send_sem=row_send.at[target, b],
             recv_sem=row_recv.at[my_mp, b],
             device_id=(my_dp, target),
@@ -145,16 +179,27 @@
 
     near = [side * half + (place + i) % half for i in range(1, half)]
     far = [(1 - side) * half + (place + i) % half for i in range(half)]
+    tail = list(enumerate(pieces))[units:]
 
     def send_near(b, carry):
         for target in near:
-            send_rows(b, target).start()
+            send_rows((b * UNIT, UNIT), b, target).start()
         return carry
 
     def send_far(b, carry):
         for target in far:
-            send_rows(b, target).start()
-        return carry
+            send_rows((b * UNIT, UNIT), b, target).start()
+        return carry
+
+    @pl.when(at_edge)
+    def _():
+        for b in range(EARLY):
+            send_rows(pieces[b], b, opposite).start()
+        pl.semaphore_wait(ready, 1)
+
+    @pl.when(my_mp == edge - 1 + 2 * side)
+    def _():
+        pl.semaphore_signal(ready, inc=1, device_id=(my_dp, edge), device_id_type=MESH)
 
     def send_id(i):
         peer = (my_dp + i) % count_dp
@@ -172,7 +217,20 @@
         return carry
 
     lax.fori_loop(0, units, send_near, 0)
-    lax.fori_loop(0, units, send_far, 0)
+    for b, piece in tail:
+        for target in near:
+            send_rows(piece, b, target).start()
+    for b in range(EARLY):
+        for target in far:
+
+            @pl.when(jnp.logical_or(jnp.logical_not(at_edge), target != opposite))
+            def _():
+                send_rows(pieces[b], b, target).start()
+
+    lax.fori_loop(EARLY, units, send_far, 0)
+    for target in far:
+        for b, piece in tail:
+            send_rows(piece, b, target).start()
     for copy in here[3:]:
         copy.wait()
     peer_ids = lax.broadcasted_iota(jnp.int32, ids_out.shape, 0)
@@ -228,12 +286,13 @@
     lax.fori_loop(1, count_dp, tile_arrives, 0)
     here[2].wait()
 
-    def rows_arrive(b, sources):
+    def rows_arrive(piece, b, sources):
+        start, size = piece
         for source in sources:
             pltpu.make_async_remote_copy(
-                src_ref=emb_ref.at[pl.ds(0, UNIT), :],
+                src_ref=emb_ref.at[pl.ds(0, size), :],
                 dst_ref=rows.at[
-                    pl.ds(pl.multiple_of(b * UNIT, UNIT), UNIT),
+                    pl.ds(pl.multiple_of(start, size), size),
                     pl.ds(pl.multiple_of(source * part, part), part),
                 ],
                 send_sem=row_send.at[source, b],
@@ -242,8 +301,7 @@
                 device_id_type=MESH,
             ).wait_recv()
 
-    def live_of(b, shape):
-        block = b // (BR // UNIT)
+    def live_of(block, shape):
         count = count_ref[block]
         column_peer = lax.broadcasted_iota(jnp.int32, shape, 1) // TR
         live = jnp.zeros(shape, jnp.int32)
@@ -253,29 +311,42 @@
             live = jnp.where(column_peer == slot, 1, live)
         return live
 
-    last_live[...] = live_of(units - 1, last_live.shape)
-
-    def score(b, carry):
-        rows_arrive(b, near + far)
-        mine = pl.ds(pl.multiple_of(b * UNIT, UNIT), UNIT)
-        live = live_of(b, (1, count_dp * TR))
+    last_live[...] = live_of(blocks - 1, last_live.shape)
+
+    def score(piece, live):
+        mine = pl.ds(pl.multiple_of(piece[0], piece[1]), piece[1])
         raw = products(rows[mine, :], pool[:, pl.ds(0, width)])
         out_ref[mine, :] = profile_of(raw, pool, width, live, scale, logits)
-        return carry
-
-    lax.fori_loop(0, units - 1, score, 0)
-    rows_arrive(units - 1, near)
-    span = width // 2
-    near_columns = pl.ds(pl.multiple_of(side * span, span), span)
-    last_near[...] = products(rows[pl.ds((units - 1) * UNIT, UNIT), near_columns], pool[:, near_columns])
-    rows_arrive(units - 1, far)
+
+    def score_unit(b, carry):
+        piece = (b * UNIT, UNIT)
+        rows_arrive(piece, b, near + far)
+        score(piece, live_of(b, (1, count_dp * TR)))
+        return carry
+
+    lax.fori_loop(0, units, score_unit, 0)
+    b, piece = tail[-1]
+    early_far = [(1 - side) * (half + 1) + i for i in range(half - 1)]
+    rows_arrive(piece, b, near + early_far)
+    last = pl.ds(*piece)
+    same = pl.ds(pl.multiple_of(side * half * part, part), half * part)
+    beyond = pl.ds(pl.multiple_of((1 - side) * (half + 1) * part, part), (half - 1) * part)
+    last_rest[...] = products(rows[last, same], pool[:, same]) + products(rows[last, beyond], pool[:, beyond])
+    for b, piece in tail[:-1]:
+        rows_arrive(piece, b, near + far)
+        score(piece, last_live[pl.ds(0, 1), :])
+    b, piece = tail[-1]
+    rows_arrive(piece, b, [opposite])
 
     def finish_rows(b, carry):
         for target in near + far:
-            send_rows(b, target).wait_send()
+            send_rows((b * UNIT, UNIT), b, target).wait_send()
         return carry
 
     lax.fori_loop(0, units, finish_rows, 0)
+    for b, piece in tail:
+        for target in near + far:
+            send_rows(piece, b, target).wait_send()
 
     def finish_ids(i, carry):
         send_id(i).wait_send()
@@ -299,20 +370,21 @@
     tile_count = centroids.shape[0] // TR
     blocks, cands = candidates.shape
     row_count = blocks * BR
-    units = row_count // UNIT
+    pieces = pieces_of(row_count)
+    last_size = pieces[-1][1]
     both = width + label_width
     slots = count_dp - 1 if count_dp <= 8 else 3
     anywhere = pl.BlockSpec(memory_space=pl.ANY)
     local = pl.BlockSpec(memory_space=pltpu.VMEM)
     scale = 2.0 / math.sqrt(width)
     handed = [
-        pltpu.VMEM((row_count - UNIT, label_width), jnp.bfloat16),
+        pltpu.VMEM((row_count - last_size, label_width), jnp.bfloat16),
         pltpu.VMEM((row_count, width), jnp.bfloat16),
         pltpu.VMEM((count_dp * TR, both), jnp.bfloat16),
         pltpu.VMEM((8, count_dp * TR), jnp.int32),
-        pltpu.VMEM((UNIT, count_dp * TR), jnp.float32),
+        pltpu.VMEM((last_size, count_dp * TR), jnp.float32),
     ]
-    handed_bytes = 2 * ((row_count - UNIT) * label_width + row_count * width) + count_dp * TR * (2 * both + 32 + 4 * UNIT)
+    handed_bytes = 2 * ((row_count - last_size) * label_width + row_count * width) + count_dp * TR * (2 * both + 32 + 4 * last_size)
     held = pl.pallas_call(
         functools.partial(kernel, count_dp, count_mp, scale),
         in_specs=[anywhere] * 6,
@@ -327,10 +399,11 @@
             pltpu.VMEM((count_dp, 8, 128), jnp.int32),
             pltpu.VMEM((count_dp, 8, 128), jnp.int32),
             pltpu.VMEM((UNIT, count_dp * TR), jnp.float32),
-            pltpu.SemaphoreType.DMA((count_mp, units)),
-            pltpu.SemaphoreType.DMA((count_mp, units)),
+            pltpu.SemaphoreType.DMA((count_mp, len(pieces))),
+            pltpu.SemaphoreType.DMA((count_mp, len(pieces))),
             pltpu.SemaphoreType.DMA((count_dp,)),
             pltpu.SemaphoreType.DMA((count_dp,)),
+            pltpu.SemaphoreType.REGULAR,
             pltpu.SemaphoreType.DMA((count_dp,)),
             pltpu.SemaphoreType.DMA((count_dp,)),
             pltpu.SemaphoreType.DMA((6,)),
@@ -353,9 +426,9 @@
         out_specs=anywhere,
         out_shape=jax.ShapeDtypeStruct((row_count, label_width), jnp.bfloat16),
         scratch_shapes=[
-            pltpu.VMEM((UNIT, count_dp * TR), jnp.float32),
-            pltpu.VMEM((UNIT, label_width), jnp.bfloat16),
-            pltpu.SemaphoreType.DMA((units,)),
+            pltpu.VMEM((last_size, count_dp * TR), jnp.float32),
+            pltpu.VMEM((last_size, label_width), jnp.bfloat16),
+            pltpu.SemaphoreType.DMA((len(pieces),)),
         ],
         compiler_params=pltpu.CompilerParams(vmem_limit_bytes=CLOSE_BYTES),
         name="close",

time: 234 us -> 234 us (level)
  no operation moved by 1% of the time
where the time goes in v1:
time: 234 us
  Pallas kernels  234 us (100%)
    pallas_call x1, Pallas kernels, body(): pl.pallas_call(functools.partial(kernel, count_dp, count_mp, scale), in_s...  231 us

profile of v1, /device:TPU:8, one launch (start us, length us, event | category | flops | bytes accessed | tf_op | source)
XLA Modules:
  0.0 233.6 jit_solution(13719492333658201506)
XLA Ops:
  0.0 231.3 %annotate.1 = (bf16[1984,1024]{1,0:T(8,128)(2,1)S(1)}, bf16[2048,2560]{1,0:T(8,128)(2,1)S(1)}, bf16[1024,3584]{1,0:T(8,128)(2,1)S(1)}, s32[8,1024]{1,0:T(8,128)S(1)}, f32[64,1024]{1,0:T(8,128)S(1)}) custom-call(s32[8,8]{1,0:T(8,128)} %cand_hbm.1, s32[8]{0:T(128)} %count_hbm.1, s32[128]{0:T(128)} %home_hbm.1, bf16[8192,640]{1,0:T(8,128)(2,1)} %emb_ref.1, ...), custom_call_target="tpu_custom_call" | custom-call | tf_op jit(solution)/shard_map/annotate/pallas_call | solution.py:388
  231.3 2.3 close.1

commit v2 on v1

--- a/solution.py
+++ b/solution.py
@@ -11,7 +11,8 @@
 TR = 128
 BR = 256
 UNIT = 256
-TAIL = (128, 64, 64)
+TAIL = (128, 128)
+ALIGN = 64
 EARLY = 2
 MESH = pl.DeviceIdType.MESH
 VMEM_BYTES = 62 * 1024 * 1024
@@ -169,8 +170,8 @@
     def send_rows(piece, b, target):
         start, size = piece
         return pltpu.make_async_remote_copy(
-            src_ref=emb_ref.at[pl.ds(pl.multiple_of(target * blocks * BR + start, size), size), :],
-            dst_ref=rows.at[pl.ds(pl.multiple_of(start, size), size), own_columns],
+            src_ref=emb_ref.at[pl.ds(pl.multiple_of(target * blocks * BR + start, ALIGN), size), :],
+            dst_ref=rows.at[pl.ds(pl.multiple_of(start, ALIGN), size), own_columns],
             send_sem=row_send.at[target, b],
             recv_sem=row_recv.at[my_mp, b],
             device_id=(my_dp, target),
@@ -292,7 +293,7 @@
             pltpu.make_async_remote_copy(
                 src_ref=emb_ref.at[pl.ds(0, size), :],
                 dst_ref=rows.at[
-                    pl.ds(pl.multiple_of(start, size), size),
+                    pl.ds(pl.multiple_of(start, ALIGN), size),
                     pl.ds(pl.multiple_of(source * part, part), part),
                 ],
                 send_sem=row_send.at[source, b],
@@ -314,7 +315,7 @@
     last_live[...] = live_of(blocks - 1, last_live.shape)
 
     def score(piece, live):
-        mine = pl.ds(pl.multiple_of(piece[0], piece[1]), piece[1])
+        mine = pl.ds(pl.multiple_of(piece[0], ALIGN), piece[1])
         raw = products(rows[mine, :], pool[:, pl.ds(0, width)])
         out_ref[mine, :] = profile_of(raw, pool, width, live, scale, logits)
 

time: 234 us -> 231 us (0.987)
  Pallas kernels: 234 us -> 231 us
    pallas_call x1, Pallas kernels: 231 us -> 229 us  [body(): pl.pallas_call(functools.partial(kernel, count_dp, count_mp, scale), in_s...]
where the time goes in v2:
time: 231 us
  Pallas kernels  231 us (100%)
    pallas_call x1, Pallas kernels, body(): pl.pallas_call(functools.partial(kernel, count_dp, count_mp, scale), in_s...  229 us

profile of v2, /device:TPU:8, one launch (start us, length us, event | category | flops | bytes accessed | tf_op | source)
XLA Modules:
  0.0 231.2 jit_solution(15618546422485343549)
XLA Ops:
  0.0 228.9 %annotate.1 = (bf16[1920,1024]{1,0:T(8,128)(2,1)S(1)}, bf16[2048,2560]{1,0:T(8,128)(2,1)S(1)}, bf16[1024,3584]{1,0:T(8,128)(2,1)S(1)}, s32[8,1024]{1,0:T(8,128)S(1)}, f32[128,1024]{1,0:T(8,128)S(1)}) custom-call(s32[8,8]{1,0:T(8,128)} %cand_hbm.1, s32[8]{0:T(128)} %count_hbm.1, s32[128]{0:T(128)} %home_hbm.1, bf16[8192,640]{1,0:T(8,128)(2,1)} %emb_ref.1, ...), custom_call_target="tpu_custom_call" | custom-call | tf_op jit(solution)/shard_map/annotate/pallas_call | solution.py:389
  228.9 2.3 close.1

commit v3 on v2

--- a/solution.py
+++ b/solution.py
@@ -13,7 +13,6 @@
 UNIT = 256
 TAIL = (128, 128)
 ALIGN = 64
-EARLY = 2
 MESH = pl.DeviceIdType.MESH
 VMEM_BYTES = 62 * 1024 * 1024
 CLOSE_BYTES = 14 * 1024 * 1024
@@ -39,8 +38,12 @@
 
 
 def pieces_of(row_count):
-    whole = row_count - sum(TAIL)
-    sizes = [UNIT] * (whole // UNIT) + list(TAIL)
+    left = row_count // UNIT
+    sizes = []
+    while left > 1:
+        sizes.append(left // 2 * UNIT)
+        left -= left // 2
+    sizes += TAIL
     starts = [sum(sizes[:i]) for i in range(len(sizes))]
     return list(zip(starts, sizes))
 
@@ -103,7 +106,7 @@
     my_mp = lax.axis_index("mp")
     blocks, cands = cand_ref.shape
     pieces = pieces_of(blocks * BR)
-    units = len(pieces) - len(TAIL)
+    bulk = len(pieces) - len(TAIL)
     part = emb_ref.shape[1]
     tile_count = stored.shape[0]
     width = cent_ref.shape[2]
@@ -180,22 +183,11 @@
 
     near = [side * half + (place + i) % half for i in range(1, half)]
     far = [(1 - side) * half + (place + i) % half for i in range(half)]
-    tail = list(enumerate(pieces))[units:]
-
-    def send_near(b, carry):
-        for target in near:
-            send_rows((b * UNIT, UNIT), b, target).start()
-        return carry
-
-    def send_far(b, carry):
-        for target in far:
-            send_rows((b * UNIT, UNIT), b, target).start()
-        return carry
+    tail = list(enumerate(pieces))[bulk:]
 
     @pl.when(at_edge)
     def _():
-        for b in range(EARLY):
-            send_rows(pieces[b], b, opposite).start()
+        send_rows(pieces[0], 0, opposite).start()
         pl.semaphore_wait(ready, 1)
 
     @pl.when(my_mp == edge - 1 + 2 * side)
@@ -217,18 +209,18 @@
         send_id(i).start()
         return carry
 
-    lax.fori_loop(0, units, send_near, 0)
-    for b, piece in tail:
+    for b, piece in enumerate(pieces):
         for target in near:
             send_rows(piece, b, target).start()
-    for b in range(EARLY):
+    for target in far:
+
+        @pl.when(jnp.logical_or(jnp.logical_not(at_edge), target != opposite))
+        def _():
+            send_rows(pieces[0], 0, target).start()
+
+    for b in range(1, bulk):
         for target in far:
-
-            @pl.when(jnp.logical_or(jnp.logical_not(at_edge), target != opposite))
-            def _():
-                send_rows(pieces[b], b, target).start()
-
-    lax.fori_loop(EARLY, units, send_far, 0)
+            send_rows(pieces[b], b, target).start()
     for target in far:
         for b, piece in tail:
             send_rows(piece, b, target).start()
@@ -320,12 +312,13 @@
         out_ref[mine, :] = profile_of(raw, pool, width, live, scale, logits)
 
     def score_unit(b, carry):
-        piece = (b * UNIT, UNIT)
+        score((b * UNIT, UNIT), live_of(b, (1, count_dp * TR)))
+        return carry
+
+    for b, piece in enumerate(pieces[:bulk]):
         rows_arrive(piece, b, near + far)
-        score(piece, live_of(b, (1, count_dp * TR)))
-        return carry
-
-    lax.fori_loop(0, units, score_unit, 0)
+        first = piece[0] // UNIT
+        lax.fori_loop(first, first + piece[1] // UNIT, score_unit, 0)
     b, piece = tail[-1]
     early_far = [(1 - side) * (half + 1) + i for i in range(half - 1)]
     rows_arrive(piece, b, near + early_far)
@@ -339,13 +332,7 @@
     b, piece = tail[-1]
     rows_arrive(piece, b, [opposite])
 
-    def finish_rows(b, carry):
-        for target in near + far:
-            send_rows((b * UNIT, UNIT), b, target).wait_send()
-        return carry
-
-    lax.fori_loop(0, units, finish_rows, 0)
-    for b, piece in tail:
+    for b, piece in enumerate(pieces):
         for target in near + far:
             send_rows(piece, b, target).wait_send()
 

time: 231 us -> 230 us (level)
  no operation moved by 1% of the time
where the time goes in v3:
time: 230 us
  Pallas kernels  230 us (100%)
    pallas_call x1, Pallas kernels, body(): pl.pallas_call(functools.partial(kernel, count_dp, count_mp, scale), in_s...  228 us

profile of v3, /device:TPU:8, one launch (start us, length us, event | category | flops | bytes accessed | tf_op | source)
XLA Modules:
  0.0 230.3 jit_solution(15917082387750720039)
XLA Ops:
  0.0 228.2 %annotate.1 = (bf16[1920,1024]{1,0:T(8,128)(2,1)S(1)}, bf16[2048,2560]{1,0:T(8,128)(2,1)S(1)}, bf16[1024,3584]{1,0:T(8,128)(2,1)S(1)}, s32[8,1024]{1,0:T(8,128)S(1)}, f32[128,1024]{1,0:T(8,128)S(1)}) custom-call(s32[8,8]{1,0:T(8,128)} %cand_hbm.1, s32[8]{0:T(128)} %count_hbm.1, s32[128]{0:T(128)} %home_hbm.1, bf16[8192,640]{1,0:T(8,128)(2,1)} %emb_ref.1, ...), custom_call_target="tpu_custom_call" | custom-call | tf_op jit(solution)/shard_map/annotate/pallas_call | solution.py:376
  228.3 2.1 close.1
